TPU v7x, 32 devices: a whole 2x2x4 slice. The times are simulated.
32 devices in a mesh: fsdp: 2 (over x), ctx: 4 (over z), tp: 4 (over y, core).
Axes of the slice: x: 2, y: 2, z: 4, core: 2. Of those that a mesh axis runs over, the one named last changes fastest.
Arguments:
- tokens: bfloat16 [4, 2048, 2048], P('fsdp', 'ctx'), may hold values from -6 to 6
- tree_position: int32 [4, 2048], P('fsdp', 'ctx'), may hold values from 0 to 2047, as said below
- segment: int32 [4, 2048], P('fsdp', 'ctx'), may hold values from 0 to 6, as said below
- parent_table: int32 [4, 7], P('fsdp'), may hold values from 0 to 2, as said below
- norm1_gain: float32 [2048], replicated, may hold values from 0.5 to 1.5
- norm1_shift: float32 [2048], replicated, may hold values from -4 to 4
- query_weight: bfloat16 [2048, 2048], P('fsdp', 'tp'), may hold values from -0.125 to 0.125
- query_bias: float32 [2048], P('tp'), may hold values from -4 to 4
- key_weight: bfloat16 [2048, 2048], P('fsdp', 'tp'), may hold values from -0.125 to 0.125
- value_weight: bfloat16 [2048, 2048], P('fsdp', 'tp'), may hold values from -0.125 to 0.125
- value_bias: float32 [2048], P('tp'), may hold values from -0.75 to 0.75
- out_weight: bfloat16 [2048, 2048], P('tp', 'fsdp'), may hold values from -1.5 to 1.5
- out_bias: float32 [2048], replicated, may hold values from -4 to 4
- norm2_gain: float32 [2048], replicated, may hold values from 0.5 to 1.5
- norm2_shift: float32 [2048], replicated, may hold values from -4 to 4
- up_weight: bfloat16 [2048, 8192], P('fsdp', 'tp'), may hold values from -0.125 to 0.125
- up_bias: float32 [8192], P('tp'), may hold values from -4 to 4
- down_weight: bfloat16 [8192, 2048], P('tp', 'fsdp'), may hold values from -0.0625 to 0.0625
- down_bias: float32 [2048], replicated, may hold values from -4 to 4
- cotangent: bfloat16 [4, 2048, 2048], P('fsdp', 'ctx'), may hold values from -6 to 6
Outputs:
- layer_out: bfloat16 [4, 2048, 2048], P('fsdp', 'ctx')
- grad_tokens: bfloat16 [4, 2048, 2048], P('fsdp', 'ctx')
- grad_norm1_gain: float32 [2048], P(('fsdp', 'ctx'))
- grad_norm1_shift: float32 [2048], P(('fsdp', 'ctx'))
- grad_query_weight: float32 [2048, 2048], P(('fsdp', 'ctx'), 'tp')
- grad_query_bias: float32 [2048], P('tp')
- grad_key_weight: float32 [2048, 2048], P(('fsdp', 'ctx'), 'tp')
- grad_value_weight: float32 [2048, 2048], P(('fsdp', 'ctx'), 'tp')
- grad_value_bias: float32 [2048], P('tp')
- grad_out_weight: float32 [2048, 2048], P('tp', ('fsdp', 'ctx'))
- grad_out_bias: float32 [2048], P(('fsdp', 'ctx'))
- grad_norm2_gain: float32 [2048], P(('fsdp', 'ctx'))
- grad_norm2_shift: float32 [2048], P(('fsdp', 'ctx'))
- grad_up_weight: float32 [2048, 8192], P(('fsdp', 'ctx'), 'tp')
- grad_up_bias: float32 [8192], P('tp')
- grad_down_weight: float32 [8192, 2048], P('tp', ('fsdp', 'ctx'))
- grad_down_bias: float32 [2048], P(('fsdp', 'ctx'))
Inputs may be any that keep to these rules, and one draw needn't show every extreme that they name: `tree_position`: within each tree the rows hold the positions 0 to 2047 once each; every aligned run of 64 rows holds 64 consecutive positions in increasing order. `segment`: along increasing positions a tree runs through segments 0 to 6 in order, each nonempty and contiguous: the trunk 0 with 1024 positions, branches 1 and 2 with 512 together, leaves 3 to 6 with 512 together. `parent_table`: entry s of a tree's row is the parent of segment s: 0 for segments 0, 1 and 2; 1 for leaf 3; 2 for leaf 6; 1 or 2 for leaves 4 and 5.
All inputs are finite; a program needn't handle non-finite values.
Results may differ from a plain program's by a relative error of at most 0.024.
Values may be sent and summed in bfloat16 or wider, within the bound.
No kernel may reach another device: no remote copies, remote signals or barrier semaphores. Data moves between devices by JAX's collectives and lax.ppermute only.
A program may use at most 256 MiB of HBM per device.

v0:
```python
from functools import partial
import math
import jax
import jax.numpy as jnp
from jax import lax
from jax.sharding import PartitionSpec as P

HD = 128
NEGATIVE = -1000000000.0


def norm_rows(values, gain, shift):
    centre = jnp.mean(values, axis=-1, keepdims=True)
    centred = values - centre
    spread = jnp.mean(centred * centred, axis=-1, keepdims=True)
    return centred * lax.rsqrt(spread + 1e-05) * gain + shift


def on_path(query_pos, query_seg, key_pos, key_seg, parent):
    labels = jnp.arange(parent.shape[0], dtype=jnp.int32)
    first = jnp.sum(jnp.where(query_seg[:, None] == labels[None, :], parent[None, :], 0), axis=1)
    second = jnp.sum(jnp.where(first[:, None] == labels[None, :], parent[None, :], 0), axis=1)
    along = (
        (key_seg[None, :] == query_seg[:, None])
        | (key_seg[None, :] == first[:, None])
        | (key_seg[None, :] == second[:, None])
    )
    return along & (key_pos[None, :] <= query_pos[:, None])


def inner_rows(left, right):
    return lax.dot_general(
        left, right, (((0,), (0,)), ((), ())), preferred_element_type=jnp.float32
    )


def times_transposed(left, right):
    return lax.dot_general(
        left, right, (((1,), (1,)), ((), ())), preferred_element_type=jnp.float32
    )


def per_device(
    tokens,
    tree_position,
    segment,
    parent_table,
    norm1_gain,
    norm1_shift,
    query_weight,
    query_bias,
    key_weight,
    value_weight,
    value_bias,
    out_weight,
    out_bias,
    norm2_gain,
    norm2_shift,
    up_weight,
    up_bias,
    down_weight,
    down_bias,
    cotangent,
):
    w_query, w_key, w_value, w_out, w_up, w_down = (
        lax.all_gather(query_weight, "fsdp", axis=0, tiled=True),
        lax.all_gather(key_weight, "fsdp", axis=0, tiled=True),
        lax.all_gather(value_weight, "fsdp", axis=0, tiled=True),
        lax.all_gather(out_weight, "fsdp", axis=1, tiled=True),
        lax.all_gather(up_weight, "fsdp", axis=0, tiled=True),
        lax.all_gather(down_weight, "fsdp", axis=1, tiled=True),
    )
    key_position, key_segment = (
        lax.all_gather(tree_position, "ctx", axis=1, tiled=True),
        lax.all_gather(segment, "ctx", axis=1, tiled=True),
    )
    local_width = w_query.shape[1]
    head_count = local_width // HD
    score_scale = 1.0 / math.sqrt(HD)
    gelu_exact = partial(jax.nn.gelu, approximate=False)
    layer_rows = []
    input_grads = []
    running = [
        jnp.zeros(w_query.shape, jnp.float32),
        jnp.zeros(w_key.shape, jnp.float32),
        jnp.zeros(w_value.shape, jnp.float32),
        jnp.zeros(w_out.shape, jnp.float32),
        jnp.zeros(w_up.shape, jnp.float32),
        jnp.zeros(w_down.shape, jnp.float32),
        jnp.zeros(norm1_gain.shape, jnp.float32),
        jnp.zeros(norm1_shift.shape, jnp.float32),
        jnp.zeros(norm2_gain.shape, jnp.float32),
        jnp.zeros(norm2_shift.shape, jnp.float32),
        jnp.zeros(out_bias.shape, jnp.float32),
        jnp.zeros(down_bias.shape, jnp.float32),
    ]
    head_sums = [
        jnp.zeros(query_bias.shape, jnp.float32),
        jnp.zeros(value_bias.shape, jnp.float32),
        jnp.zeros(up_bias.shape, jnp.float32),
    ]
    for batch_index in range(tokens.shape[0]):
        inputs = tokens[batch_index].astype(jnp.float32)
        local_rows = inputs.shape[0]
        normed = norm_rows(inputs, norm1_gain, norm1_shift).astype(jnp.bfloat16)
        queries = (
            jnp.dot(normed, w_query, preferred_element_type=jnp.float32) + query_bias
        ).astype(jnp.bfloat16)
        keys_local = jnp.dot(normed, w_key, preferred_element_type=jnp.float32).astype(jnp.bfloat16)
        values_local = (
            jnp.dot(normed, w_value, preferred_element_type=jnp.float32) + value_bias
        ).astype(jnp.bfloat16)
        keys_tree, values_tree = (
            lax.all_gather(keys_local, "ctx", axis=0, tiled=True),
            lax.all_gather(values_local, "ctx", axis=0, tiled=True),
        )
        tree_rows = keys_tree.shape[0]
        visible = on_path(
            tree_position[batch_index],
            segment[batch_index],
            key_position[batch_index],
            key_segment[batch_index],
            parent_table[batch_index],
        )
        query_heads = queries.reshape(local_rows, head_count, HD)
        key_heads = keys_tree.reshape(tree_rows, head_count, HD)
        value_heads = values_tree.reshape(tree_rows, head_count, HD)
        scores = (
            jnp.einsum("qhd,khd->hqk", query_heads, key_heads, preferred_element_type=jnp.float32)
            * score_scale
        )
        scores = jnp.where(visible[None], scores, NEGATIVE)
        row_max = jnp.max(scores, axis=-1, keepdims=True)
        shifted = jnp.exp(scores - row_max)
        row_total = jnp.sum(shifted, axis=-1, keepdims=True)
        log_total = row_max + jnp.log(row_total)
        soft_low = (shifted / row_total).astype(jnp.bfloat16)
        attended = (
            jnp.einsum("hqk,khd->qhd", soft_low, value_heads, preferred_element_type=jnp.float32)
            .reshape(local_rows, local_width)
            .astype(jnp.bfloat16)
        )
        middle = inputs + (
            lax.psum(
                jnp.dot(attended, w_out, preferred_element_type=jnp.float32).astype(jnp.bfloat16),
                "tp",
            ).astype(jnp.float32)
            + out_bias
        )
        normed_mid = norm_rows(middle, norm2_gain, norm2_shift).astype(jnp.bfloat16)
        hidden = jnp.dot(normed_mid, w_up, preferred_element_type=jnp.float32) + up_bias
        active = gelu_exact(hidden).astype(jnp.bfloat16)
        result = middle + (
            lax.psum(
                jnp.dot(active, w_down, preferred_element_type=jnp.float32).astype(jnp.bfloat16),
                "tp",
            ).astype(jnp.float32)
            + down_bias
        )
        layer_rows.append(result.astype(jnp.bfloat16))
        grad_out = cotangent[batch_index]
        grad_float = grad_out.astype(jnp.float32)
        down_bias_term = jnp.sum(grad_float, axis=0)
        down_term = inner_rows(active, grad_out)
        _, gelu_pull = jax.vjp(gelu_exact, hidden)
        grad_hidden = gelu_pull(times_transposed(grad_out, w_down))[0].astype(jnp.bfloat16)
        up_bias_term = jnp.sum(grad_hidden.astype(jnp.float32), axis=0)
        up_term = inner_rows(normed_mid, grad_hidden)
        grad_normed_mid = lax.psum(
            times_transposed(grad_hidden, w_up).astype(jnp.bfloat16), "tp"
        ).astype(jnp.float32)
        _, second_pull = jax.vjp(norm_rows, middle, norm2_gain, norm2_shift)
        grad_mid_norm, second_gain_term, second_shift_term = second_pull(grad_normed_mid)
        grad_middle = grad_float + grad_mid_norm
        grad_branch = grad_middle.astype(jnp.bfloat16)
        out_bias_term = jnp.sum(grad_branch.astype(jnp.float32), axis=0)
        out_term = inner_rows(attended, grad_branch)
        grad_attended = times_transposed(grad_branch, w_out).astype(jnp.bfloat16)
        grad_heads = grad_attended.reshape(local_rows, head_count, HD)
        again = (
            jnp.einsum("qhd,khd->hqk", query_heads, key_heads, preferred_element_type=jnp.float32)
            * score_scale
        )
        again = jnp.where(visible[None], again, NEGATIVE)
        soft = jnp.exp(again - log_total)
        soft_again = soft.astype(jnp.bfloat16)
        grad_soft = jnp.einsum(
            "qhd,khd->hqk", grad_heads, value_heads, preferred_element_type=jnp.float32
        )
        inner = jnp.sum(soft * grad_soft, axis=-1, keepdims=True)
        grad_scores = (soft * (grad_soft - inner)).astype(jnp.bfloat16)
        grad_queries = (
            (
                jnp.einsum(
                    "hqk,khd->qhd", grad_scores, key_heads, preferred_element_type=jnp.float32
                )
                * score_scale
            )
            .reshape(local_rows, local_width)
            .astype(jnp.bfloat16)
        )
        key_part = (
            jnp.einsum("hqk,qhd->khd", grad_scores, query_heads, preferred_element_type=jnp.float32)
            * score_scale
        ).reshape(tree_rows, local_width)
        value_part = jnp.einsum(
            "hqk,qhd->khd", soft_again, grad_heads, preferred_element_type=jnp.float32
        ).reshape(tree_rows, local_width)
        grad_keys, grad_values = (
            lax.psum_scatter(
                key_part.astype(jnp.bfloat16), "ctx", scatter_dimension=0, tiled=True
            ).astype(jnp.float32),
            lax.psum_scatter(
                value_part.astype(jnp.bfloat16), "ctx", scatter_dimension=0, tiled=True
            ).astype(jnp.float32),
        )
        grad_keys = grad_keys.astype(jnp.bfloat16)
        grad_values = grad_values.astype(jnp.bfloat16)
        query_bias_term = jnp.sum(grad_queries.astype(jnp.float32), axis=0)
        value_bias_term = jnp.sum(grad_values.astype(jnp.float32), axis=0)
        query_term = inner_rows(normed, grad_queries)
        key_term = inner_rows(normed, grad_keys)
        value_term = inner_rows(normed, grad_values)
        grad_normed = lax.psum(
            (
                times_transposed(grad_queries, w_query)
                + times_transposed(grad_keys, w_key)
                + times_transposed(grad_values, w_value)
            ).astype(jnp.bfloat16),
            "tp",
        ).astype(jnp.float32)
        _, first_pull = jax.vjp(norm_rows, inputs, norm1_gain, norm1_shift)
        grad_in_norm, first_gain_term, first_shift_term = first_pull(grad_normed)
        input_grads.append((grad_middle + grad_in_norm).astype(jnp.bfloat16))
        head_sums = [
            head_sums[0] + query_bias_term,
            head_sums[1] + value_bias_term,
            head_sums[2] + up_bias_term,
        ]
        fresh = [
            query_term,
            key_term,
            value_term,
            out_term,
            up_term,
            down_term,
            first_gain_term,
            first_shift_term,
            second_gain_term,
            second_shift_term,
            out_bias_term,
            down_bias_term,
        ]
        running = [older + newer for older, newer in zip(running, fresh)]
    final = (
        lax.psum_scatter(
            running[0].astype(jnp.bfloat16), ("fsdp", "ctx"), scatter_dimension=0, tiled=True
        ).astype(jnp.float32),
        lax.psum_scatter(
            running[1].astype(jnp.bfloat16), ("fsdp", "ctx"), scatter_dimension=0, tiled=True
        ).astype(jnp.float32),
        lax.psum_scatter(
            running[2].astype(jnp.bfloat16), ("fsdp", "ctx"), scatter_dimension=0, tiled=True
        ).astype(jnp.float32),
        lax.psum_scatter(
            running[3].astype(jnp.bfloat16), ("fsdp", "ctx"), scatter_dimension=1, tiled=True
        ).astype(jnp.float32),
        lax.psum_scatter(
            running[4].astype(jnp.bfloat16), ("fsdp", "ctx"), scatter_dimension=0, tiled=True
        ).astype(jnp.float32),
        lax.psum_scatter(
            running[5].astype(jnp.bfloat16), ("fsdp", "ctx"), scatter_dimension=1, tiled=True
        ).astype(jnp.float32),
        lax.psum_scatter(
            running[6].astype(jnp.bfloat16), ("fsdp", "ctx"), scatter_dimension=0, tiled=True
        ).astype(jnp.float32),
        lax.psum_scatter(
            running[7].astype(jnp.bfloat16), ("fsdp", "ctx"), scatter_dimension=0, tiled=True
        ).astype(jnp.float32),
        lax.psum_scatter(
            running[8].astype(jnp.bfloat16), ("fsdp", "ctx"), scatter_dimension=0, tiled=True
        ).astype(jnp.float32),
        lax.psum_scatter(
            running[9].astype(jnp.bfloat16), ("fsdp", "ctx"), scatter_dimension=0, tiled=True
        ).astype(jnp.float32),
        lax.psum_scatter(
            running[10].astype(jnp.bfloat16), ("fsdp", "ctx"), scatter_dimension=0, tiled=True
        ).astype(jnp.float32),
        lax.psum_scatter(
            running[11].astype(jnp.bfloat16), ("fsdp", "ctx"), scatter_dimension=0, tiled=True
        ).astype(jnp.float32),
    )
    bias_totals = lax.psum((head_sums[0], head_sums[1], head_sums[2]), ("fsdp", "ctx"))
    return (
        jnp.stack(layer_rows),
        jnp.stack(input_grads),
        final[6],
        final[7],
        final[0],
        bias_totals[0],
        final[1],
        final[2],
        bias_totals[1],
        final[3],
        final[10],
        final[8],
        final[9],
        final[4],
        bias_totals[2],
        final[5],
        final[11],
    )


def solution(mesh):
    in_specs = (
        P("fsdp", "ctx", None),
        P("fsdp", "ctx"),
        P("fsdp", "ctx"),
        P("fsdp", None),
        P(),
        P(),
        P("fsdp", "tp"),
        P("tp"),
        P("fsdp", "tp"),
        P("fsdp", "tp"),
        P("tp"),
        P("tp", "fsdp"),
        P(),
        P(),
        P(),
        P("fsdp", "tp"),
        P("tp"),
        P("tp", "fsdp"),
        P(),
        P("fsdp", "ctx", None),
    )
    out_specs = (
        P("fsdp", "ctx", None),
        P("fsdp", "ctx", None),
        P(("fsdp", "ctx")),
        P(("fsdp", "ctx")),
        P(("fsdp", "ctx"), "tp"),
        P("tp"),
        P(("fsdp", "ctx"), "tp"),
        P(("fsdp", "ctx"), "tp"),
        P("tp"),
        P("tp", ("fsdp", "ctx")),
        P(("fsdp", "ctx")),
        P(("fsdp", "ctx")),
        P(("fsdp", "ctx")),
        P(("fsdp", "ctx"), "tp"),
        P("tp"),
        P("tp", ("fsdp", "ctx")),
        P(("fsdp", "ctx")),
    )
    return jax.shard_map(
        per_device, mesh=mesh, in_specs=in_specs, out_specs=out_specs, check_vma=False
    )
```

profile of v0, /device:TPU:0, one launch (start us, length us, event | category | flops | bytes accessed | tf_op | source)
XLA Modules:
  0.0 1765.6 jit_solution(16813001893812341595)
XLA Ops:
  14.5 30.9 %all-gather.17.cloned.1.call-done = bf16[2048,512]{1,0:T(8,128)(2,1)} async-done(((bf16[1024,512]{1,0:T(8,128)(2,1)}), bf16[2048,512]{1,0:T(8,128)(2,1)}) %all-gather.17.cloned.1.call-update) | async-done | bytes 2097168 | tf_op jit(solution)/shard_map/all_gather | solution.py:67
  49.2 30.9 %all-gather.11.cloned.1.call-done = bf16[2048,512]{1,0:T(8,128)(2,1)} async-done(((bf16[1024,512]{1,0:T(8,128)(2,1)}), bf16[2048,512]{1,0:T(8,128)(2,1)}) %all-gather.11.cloned.1.call-update) | async-done | bytes 2097168 | tf_op jit(solution)/shard_map/all_gather | solution.py:68
  84.4 13.3 all_gather.39
  97.6 13.4 all_gather.38
  118.4 44.0 %all-gather.19.cloned.1.call-done = bf16[2048,512]{1,0:T(8,128)(2,1)} async-done(((bf16[512,512]{1,0:T(8,128)(2,1)}), bf16[2048,512]{1,0:T(8,128)(2,1)}) %all-gather.19.cloned.1.call-update) | async-done | bytes 2097168 | tf_op jit(solution)/shard_map/all_gather | solution.py:114
  165.4 9.3 fusion.162
  174.7 8.2 fusion
  182.8 26.1 %all-gather.13.cloned.1.call-done = bf16[2048,512]{1,0:T(8,128)(2,1)} async-done(((bf16[512,512]{1,0:T(8,128)(2,1)}), bf16[2048,512]{1,0:T(8,128)(2,1)}) %all-gather.13.cloned.1.call-update) | async-done | bytes 2097168 | tf_op jit(solution)/shard_map/all_gather | solution.py:115
  208.9 8.5 fusion.127
  217.4 24.8 %all-gather.21.cloned.1.call-done = bf16[512,2048]{1,0:T(8,128)(2,1)} async-done(((bf16[512,1024]{1,0:T(8,128)(2,1)}), bf16[512,2048]{1,0:T(8,128)(2,1)}) %all-gather.21.cloned.1.call-update) | async-done | bytes 2097168 | tf_op jit(solution)/shard_map/all_gather | solution.py:69
  246.9 51.0 %all-reduce.15.cloned.1.call-done = bf16[512,2048]{1,0:T(8,128)(2,1)} async-done(((bf16[512,2048]{1,0:T(8,128)(2,1)}), bf16[512,2048]{1,0:T(8,128)(2,1)}) %all-reduce.15.cloned.1.call-update) | async-done | bytes 2097168 | tf_op jit(solution)/shard_map/psum | solution.py:144
  317.3 35.4 %all-gather.29.cloned.1.call-done = bf16[2048,512]{1,0:T(8,128)(2,1)} async-done(((bf16[512,512]{1,0:T(8,128)(2,1)}), bf16[2048,512]{1,0:T(8,128)(2,1)}) %all-gather.29.cloned.1.call-update) | async-done | bytes 2097168 | tf_op jit(solution)/shard_map/all_gather | solution.py:114
  355.6 9.5 fusion.163
  365.0 8.2 fusion.1
  373.2 26.0 %all-gather.27.cloned.1.call-done = bf16[2048,512]{1,0:T(8,128)(2,1)} async-done(((bf16[512,512]{1,0:T(8,128)(2,1)}), bf16[2048,512]{1,0:T(8,128)(2,1)}) %all-gather.27.cloned.1.call-update) | async-done | bytes 2097168 | tf_op jit(solution)/shard_map/all_gather | solution.py:115
  399.3 8.3 fusion.124
  412.6 48.8 %all-reduce.17.cloned.1.call-done = bf16[512,2048]{1,0:T(8,128)(2,1)} async-done(((bf16[512,2048]{1,0:T(8,128)(2,1)}), bf16[512,2048]{1,0:T(8,128)(2,1)}) %all-reduce.17.cloned.1.call-update) | async-done | bytes 2097168 | tf_op jit(solution)/shard_map/psum | solution.py:144
  467.8 99.3 %all-gather.23.cloned.1.call-done = bf16[2048,2048]{1,0:T(8,128)(2,1)} async-done(((bf16[1024,2048]{1,0:T(8,128)(2,1)}), bf16[2048,2048]{1,0:T(8,128)(2,1)}) %all-gather.23.cloned.1.call-update) | async-done | bytes 8388624 | tf_op jit(solution)/shard_map/all_gather | solution.py:70
  567.1 8.0 fusion.142
  577.3 26.2 %multiply_convert_fusion.5 = (bf16[512,2048]{1,0:T(8,128)(2,1)}, f32[512,2048]{1,0:T(8,128)}, bf16[512,2048]{1,0:T(8,128)(2,1)}, f32[512,2048]{1,0:T(8,128)}, f32[512,2048]{1,0:T(8,128)}) fusion(f32[2048]{0:T(1024)S(1)} %copy-done.101, f32[512,2048]{1,0:T(8,128)S(1)} %fusion.142, bf16[2048,2048]{1,0:T(8,128)(2,1)S(1)} %copy-done.99, ...), kind=kOutput, calls=%fused_computation.131 | convolution fusion | flops 4442816512 | bytes 33591296 | tf_op jit(solution)/shard_map/dot_general | solution.py:151
  603.5 68.9 %all-gather.25.cloned.1.call-done = bf16[2048,2048]{1,0:T(8,128)(2,1)} async-done(((bf16[2048,1024]{1,0:T(8,128)(2,1)}), bf16[2048,2048]{1,0:T(8,128)(2,1)}) %all-gather.25.cloned.1.call-update) | async-done | bytes 8388624 | tf_op jit(solution)/shard_map/all_gather | solution.py:71
  672.5 14.2 convert_reduce_fusion.8
  686.6 10.0 convolution_convert_fusion
  696.6 12.2 convert_reduce_fusion.9
  708.8 9.9 convolution_convert_fusion.1
  719.4 85.0 %all-reduce.21.cloned.1.call-done = (bf16[512,2048]{1,0:T(8,128)(2,1)}, bf16[512,2048]{1,0:T(8,128)(2,1)}) async-done(((bf16[512,2048]{1,0:T(8,128)(2,1)}, bf16[512,2048]{1,0:T(8,128)(2,1)}), (bf16[512,2048]{1,0:T(8,128)(2,1)}, bf16[512,2048]{1,0:T(8,128)(2,1)})) %all-reduce.21.cloned.1.call-update) | async-done | bytes 4194320 | tf_op jit(solution)/shard_map/psum | solution.py:169
  817.3 8.8 convert_reduce_fusion.10
  837.1 10.7 fusion.73
  847.9 11.3 multiply_reduce_fusion.1
  859.2 12.0 multiply_convert_fusion.1
  875.6 11.5 multiply_reduce_fusion
  887.1 11.9 multiply_convert_fusion
  936.5 31.4 %reduce-scatter.11.cloned.1.call-done = bf16[512,512]{0,1:T(8,128)(2,1)} async-done(((bf16[2048,512]{0,1:T(8,128)(2,1)}), bf16[512,512]{0,1:T(8,128)(2,1)}) %reduce-scatter.11.cloned.1.call-update) | async-done | bytes 524304 | tf_op jit(solution)/shard_map/reduce_scatter | solution.py:210
  972.3 40.7 %reduce-scatter.15.cloned.1.call-done = bf16[512,512]{0,1:T(8,128)(2,1)} async-done(((bf16[2048,512]{0,1:T(8,128)(2,1)}), bf16[512,512]{0,1:T(8,128)(2,1)}) %reduce-scatter.15.cloned.1.call-update) | async-done | bytes 524304 | tf_op jit(solution)/shard_map/reduce_scatter | solution.py:210
  1019.1 9.2 convolution_convert_fusion.4
  1028.3 9.3 convolution_convert_fusion.2
  1049.6 13.8 fusion.140
  1063.4 15.7 add_convert_fusion.1
  1080.7 9.9 fusion.98
  1090.6 11.0 add_convert_fusion
  1108.8 46.7 %reduce-scatter.19.cloned.1.call-done = bf16[256,512]{1,0:T(8,128)(2,1)} async-done(((bf16[2048,512]{1,0:T(8,128)(2,1)}), bf16[256,512]{1,0:T(8,128)(2,1)}) %reduce-scatter.19.cloned.1.call-update) | async-done | bytes 262160 | tf_op jit(solution)/shard_map/reduce_scatter | solution.py:256
  1157.3 35.1 %all-reduce.6 = (f32[512]{0:T(512)}, f32[512]{0:T(512)}, f32[2048]{0:T(1024)}) all-reduce(f32[512]{0:T(512)S(1)} %add_bitcast_fusion, f32[512]{0:T(512)S(1)} %add.353, f32[2048]{0:T(1024)S(1)} %add.359), channel_id=1, replica_groups=mesh['fsdp'=2,'ctx'=4,'tp'=4] {'fsdp','ctx'}, use_global_device_ids=true, to_apply=%region_47.48 | all-reduce | flops 3072 | bytes 24576 | tf_op jit(solution)/shard_map/psum | solution.py:293
  1192.4 34.0 %reduce-scatter.23.cloned.1.call-done = bf16[256,512]{1,0:T(8,128)(2,1)} async-done(((bf16[2048,512]{1,0:T(8,128)(2,1)}), bf16[256,512]{1,0:T(8,128)(2,1)}) %reduce-scatter.23.cloned.1.call-update) | async-done | bytes 262160 | tf_op jit(solution)/shard_map/reduce_scatter | solution.py:262
  1228.2 69.2 %reduce-scatter.21.cloned.1.call-done = bf16[256,512]{1,0:T(8,128)(2,1)} async-done(((bf16[2048,512]{1,0:T(8,128)(2,1)}), bf16[256,512]{1,0:T(8,128)(2,1)}) %reduce-scatter.21.cloned.1.call-update) | async-done | bytes 262160 | tf_op jit(solution)/shard_map/reduce_scatter | solution.py:259
  1299.2 153.4 %all-reduce.19.cloned.1.call-done = (bf16[512,2048]{1,0:T(8,128)(2,1)}, bf16[512,2048]{1,0:T(8,128)(2,1)}, bf16[512,2048]{1,0:T(8,128)(2,1)}, bf16[512,2048]{1,0:T(8,128)(2,1)}) async-done(((bf16[512,2048]{1,0:T(8,128)(2,1)}, bf16[512,2048]{1,0:T(8,128)(2,1)}, bf16[512,2048]{1,0:T(8,128)(2,1)}, bf16[512,2048]{1,0:T(8,128)(2,1)}), (bf16[512,2048]{1,0:T(8,128)(2,1)}, bf16[512,2048]{1,0:T(8,128)(2,1)}, ...) | async-done | bytes 8388624 | tf_op jit(solution)/shard_map/psum | solution.py:154
  1462.6 40.6 %all-reduce.7 = (bf16[2048]{0:T(1024)(128)(2,1)S(1)}, bf16[2048]{0:T(1024)(128)(2,1)S(1)}, bf16[2048]{0:T(1024)(128)(2,1)S(1)}, bf16[2048]{0:T(1024)(128)(2,1)S(...) all-reduce(bf16[2048]{0:T(1024)(128)(2,1)S(1)} %add_convert_fusion., ...), channel_id=6, replica_groups=mesh['fsdp'=2,'ctx'=4,'tp'=4] {'fsdp','ctx'}, use_global_device_ids=true, to_apply=%region_40.41.clone | all-reduce | flops 12288 | bytes 49152
  1525.9 79.1 %reduce-scatter.27.cloned.1.call-done = bf16[256,2048]{1,0:T(8,128)(2,1)} async-done(((bf16[2048,2048]{1,0:T(8,128)(2,1)}), bf16[256,2048]{1,0:T(8,128)(2,1)}) %reduce-scatter.27.cloned.1.call-update) | async-done | bytes 1048592 | tf_op jit(solution)/shard_map/reduce_scatter | solution.py:268
  1607.9 147.7 %reduce-scatter.29.cloned.1.call-done = bf16[2048,256]{1,0:T(8,128)(2,1)} async-done(((bf16[2048,2048]{1,0:T(8,128)(2,1)}), bf16[2048,256]{1,0:T(8,128)(2,1)}) %reduce-scatter.29.cloned.1.call-update) | async-done | bytes 1048592 | tf_op jit(solution)/shard_map/reduce_scatter | solution.py:271
  (383 shorter events, 205.5 us)
Async XLA Ops:
  7.2 38.2 %all-gather.17.cloned.1.call-start = ((), (), s32[]{:S(2)}) async-start(), calls=%async_computation.13 | async-start | bytes 3145728 | tf_op jit(solution)/shard_map/all_gather | solution.py:67
  7.9 72.1 %all-gather.11.cloned.1.call-start = ((), (), s32[]{:S(2)}) async-start(), calls=%async_computation.10 | async-start | bytes 3145728 | tf_op jit(solution)/shard_map/all_gather | solution.py:68
  8.7 106.0 %all-gather.15.cloned.1.call-start = ((), (), s32[]{:S(2)}) async-start(), calls=%async_computation.12 | async-start | bytes 3145728 | tf_op jit(solution)/shard_map/all_gather | solution.py:66
  9.4 153.0 %all-gather.19.cloned.1.call-start = ((), (), s32[]{:S(2)}) async-start(), calls=%async_computation.14 | async-start | bytes 2621440 | tf_op jit(solution)/shard_map/all_gather | solution.py:114
  12.9 36.1 %copy-start.61 = (f32[512]{0:T(512)}, f32[512]{0:T(512)S(1)}, u32[]{:S(2)}) copy-start(f32[512]{0:T(512)S(1)} %broadcast_multiply_fusion.3) | copy-start | bytes 6148
  13.6 35.4 %copy-start.90 = (f32[512]{0:T(512)}, f32[512]{0:T(512)S(1)}, u32[]{:S(2)}) copy-start(f32[512]{0:T(512)S(1)} %fusion.40) | copy-start | bytes 6148
  13.7 35.4 %copy-start.68 = (f32[512]{0:T(512)}, f32[512]{0:T(512)S(1)}, u32[]{:S(2)}) copy-start(f32[512]{0:T(512)S(1)} %fusion.134) | copy-start | bytes 6148
  14.5 100.2 %copy-start.27 = (bf16[512,2048]{1,0:T(8,128)(2,1)}, bf16[512,2048]{1,0:T(8,128)(2,1)S(1)}, u32[]{:S(2)}) copy-start(bf16[512,2048]{1,0:T(8,128)(2,1)S(1)} %fusion.33) | copy-start | bytes 6291460
  14.5 65.5 %copy-start.104 = (f32[512]{0:T(512)S(1)}, f32[512]{0:T(512)}, u32[]{:S(2)}) copy-start(f32[512]{0:T(512)} %param.30) | copy-start | bytes 6148
  49.1 35.3 %copy-start.92 = (s32[2,512]{1,0:T(2,128)S(1)}, s32[2,512]{1,0:T(2,128)}, u32[]{:S(2)}) copy-start(s32[2,512]{1,0:T(2,128)} %param.21) | copy-start | bytes 12292
  49.1 48.6 %copy-start.93 = (s32[2,512]{1,0:T(2,128)S(1)}, s32[2,512]{1,0:T(2,128)}, u32[]{:S(2)}) copy-start(s32[2,512]{1,0:T(2,128)} %param.22) | copy-start | bytes 12292
  49.1 62.0 %copy-start.98 = (s32[2,7]{1,0:T(2,128)S(1)}, s32[2,7]{1,0:T(2,128)}, u32[]{:S(2)}) copy-start(s32[2,7]{1,0:T(2,128)} %param.23) | copy-start | bytes 172
  49.1 65.6 %copy-start.105 = (f32[512]{0:T(512)S(1)}, f32[512]{0:T(512)}, u32[]{:S(2)}) copy-start(f32[512]{0:T(512)} %param.27) | copy-start | bytes 6148
  49.1 159.8 %all-gather.13.cloned.1.call-start = ((), (), s32[]{:S(2)}) async-start(), calls=%async_computation.11 | async-start | bytes 2621440 | tf_op jit(solution)/shard_map/all_gather | solution.py:115
  83.7 158.5 %all-gather.21.cloned.1.call-start = ((), (), s32[]{:S(2)}) async-start(), calls=%async_computation.15 | async-start | bytes 3145728 | tf_op jit(solution)/shard_map/all_gather | solution.py:69
  84.3 213.7 %all-reduce.15.cloned.1.call-start = ((), (), s32[]{:S(2)}) async-start(), calls=%async_computation.16 | async-start | bytes 4194304 | tf_op jit(solution)/shard_map/psum | solution.py:144
  182.8 34.6 %copy-start.66 = (f32[4,512]{1,0:T(4,128)}, f32[4,512]{1,0:T(4,128)S(1)}, u32[]{:S(2)}) copy-start(f32[4,512]{1,0:T(4,128)S(1)} %fusion) | copy-start | bytes 24580
  217.4 84.9 %copy-start.52 = (bf16[4,128,512]{2,1,0:T(8,128)(2,1)}, bf16[4,128,512]{2,1,0:T(8,128)(2,1)S(1)}, u32[]{:S(2)}) copy-start(bf16[4,128,512]{2,1,0:T(8,128)(2,1)S(1)} %fusion.127) | copy-start | bytes 1572868
  217.4 80.6 %copy-start.51 = (f32[2048]{0:T(1024)S(1)}, f32[2048]{0:T(1024)}, u32[]{:S(2)}) copy-start(f32[2048]{0:T(1024)} %param.32) | copy-start | bytes 24580
  246.5 106.1 %all-gather.29.cloned.1.call-start = ((), (), s32[]{:S(2)}) async-start(), calls=%async_computation.20 | async-start | bytes 2621440 | tf_op jit(solution)/shard_map/all_gather | solution.py:114
  246.9 65.5 %copy-start.63 = (f32[512]{0:T(512)}, f32[512]{0:T(512)S(1)}, u32[]{:S(2)}) copy-start(f32[512]{0:T(512)S(1)} %broadcast_multiply_fusion.1) | copy-start | bytes 6148
  306.7 92.5 %all-gather.27.cloned.1.call-start = ((), (), s32[]{:S(2)}) async-start(), calls=%async_computation.19 | async-start | bytes 2621440 | tf_op jit(solution)/shard_map/all_gather | solution.py:115
  310.5 150.9 %all-reduce.17.cloned.1.call-start = ((), (), s32[]{:S(2)}) async-start(), calls=%async_computation.21 | async-start | bytes 4194304 | tf_op jit(solution)/shard_map/psum | solution.py:144
  373.2 35.2 %copy-start.100 = (bf16[512,2048]{1,0:T(8,128)(2,1)S(1)}, bf16[512,2048]{1,0:T(8,128)(2,1)}, u32[]{:S(2)}) copy-start(bf16[512,2048]{1,0:T(8,128)(2,1)} %all-gather.21.cloned.1.call-done) | copy-start | bytes 6291460
  411.0 156.0 %all-gather.23.cloned.1.call-start = ((), (), s32[]{:S(2)}) async-start(), calls=%async_computation.17 | async-start | bytes 12582912 | tf_op jit(solution)/shard_map/all_gather | solution.py:70
  411.8 260.7 %all-gather.25.cloned.1.call-start = ((), (), s32[]{:S(2)}) async-start(), calls=%async_computation.18 | async-start | bytes 12582912 | tf_op jit(solution)/shard_map/all_gather | solution.py:71
  412.3 392.0 %all-reduce.21.cloned.1.call-start = ((), (), s32[]{:S(2)}) async-start(), calls=%async_computation.33 | async-start | bytes 8388608 | tf_op jit(solution)/shard_map/psum | solution.py:169
  465.9 101.2 %copy-start.56 = (f32[2048]{0:T(1024)S(1)}, f32[2048]{0:T(1024)}, u32[]{:S(2)}) copy-start(f32[2048]{0:T(1024)} %param.33) | copy-start | bytes 24580
  465.9 101.2 %copy-start.102 = (f32[2048]{0:T(1024)S(1)}, f32[2048]{0:T(1024)}, u32[]{:S(2)}) copy-start(f32[2048]{0:T(1024)} %param.34) | copy-start | bytes 24580
  465.9 351.3 %copy-start.59 = (f32[512]{0:T(512)}, f32[512]{0:T(512)S(1)}, u32[]{:S(2)}) copy-start(f32[512]{0:T(512)S(1)} %get-tuple-element.104) | copy-start | bytes 6148
  467.8 349.4 %copy-start.74 = (f32[512]{0:T(512)}, f32[512]{0:T(512)S(1)}, u32[]{:S(2)}) copy-start(f32[512]{0:T(512)S(1)} %fusion.137) | copy-start | bytes 6148
  467.8 109.5 %copy-start.101 = (f32[2048]{0:T(1024)S(1)}, f32[2048]{0:T(1024)}, u32[]{:S(2)}) copy-start(f32[2048]{0:T(1024)} %param.36) | copy-start | bytes 24580
  718.7 207.5 %reduce-scatter.13.cloned.1.call-start = ((), (), s32[]{:S(2)}) async-start(), calls=%async_computation.23 | async-start | bytes 2621440 | tf_op jit(solution)/shard_map/reduce_scatter | solution.py:213
  834.0 96.5 %reduce-scatter.17.cloned.1.call-start = ((), (), s32[]{:S(2)}) async-start(), calls=%async_computation.25 | async-start | bytes 2621440 | tf_op jit(solution)/shard_map/reduce_scatter | solution.py:213
  847.8 120.1 %reduce-scatter.11.cloned.1.call-start = ((), (), s32[]{:S(2)}) async-start(), calls=%async_computation.22 | async-start | bytes 2621440 | tf_op jit(solution)/shard_map/reduce_scatter | solution.py:210
  875.5 137.4 %reduce-scatter.15.cloned.1.call-start = ((), (), s32[]{:S(2)}) async-start(), calls=%async_computation.24 | async-start | bytes 2621440 | tf_op jit(solution)/shard_map/reduce_scatter | solution.py:210
  903.5 203.5 %reduce-scatter.25.cloned.1.call-start = ((), (), s32[]{:S(2)}) async-start(), calls=%async_computation.29 | async-start | bytes 2359296 | tf_op jit(solution)/shard_map/reduce_scatter | solution.py:265
  908.0 247.5 %reduce-scatter.19.cloned.1.call-start = ((), (), s32[]{:S(2)}) async-start(), calls=%async_computation.26 | async-start | bytes 2359296 | tf_op jit(solution)/shard_map/reduce_scatter | solution.py:256
  926.1 300.4 %reduce-scatter.23.cloned.1.call-start = ((), (), s32[]{:S(2)}) async-start(), calls=%async_computation.28 | async-start | bytes 2359296 | tf_op jit(solution)/shard_map/reduce_scatter | solution.py:262
  936.5 361.0 %reduce-scatter.21.cloned.1.call-start = ((), (), s32[]{:S(2)}) async-start(), calls=%async_computation.27 | async-start | bytes 2359296 | tf_op jit(solution)/shard_map/reduce_scatter | solution.py:259
  972.3 46.8 %copy-start.107 = (bf16[512,2048]{1,0:T(8,128)(2,1)S(1)}, bf16[512,2048]{1,0:T(8,128)(2,1)}, u32[]{:S(2)}) copy-start(bf16[512,2048]{1,0:T(8,128)(2,1)} %get-tuple-element.64) | copy-start | bytes 6291460
  1018.8 433.8 %all-reduce.19.cloned.1.call-start = ((), (), s32[]{:S(2)}) async-start(), calls=%async_computation.32 | async-start | bytes 16777216 | tf_op jit(solution)/shard_map/psum | solution.py:154
  1048.9 556.1 %reduce-scatter.27.cloned.1.call-start = ((), (), s32[]{:S(2)}) async-start(), calls=%async_computation.30 | async-start | bytes 9437184 | tf_op jit(solution)/shard_map/reduce_scatter | solution.py:268
  1079.1 676.5 %reduce-scatter.29.cloned.1.call-start = ((), (), s32[]{:S(2)}) async-start(), calls=%async_computation.31 | async-start | bytes 9437184 | tf_op jit(solution)/shard_map/reduce_scatter | solution.py:271
  1458.5 48.5 %copy-start.15 = (bf16[512,2048]{1,0:T(8,128)(2,1)S(1)}, bf16[512,2048]{1,0:T(8,128)(2,1)}, u32[]{:S(2)}) copy-start(bf16[512,2048]{1,0:T(8,128)(2,1)} %all-reduce.15.cloned.1.call-done) | copy-start | bytes 6291460
  1458.6 48.5 %copy-start.65 = (f32[2048]{0:T(1024)S(1)}, f32[2048]{0:T(1024)}, u32[]{:S(2)}) copy-start(f32[2048]{0:T(1024)} %param.38) | copy-start | bytes 24580
  1458.6 48.5 %copy-start.73 = (f32[512]{0:T(512)S(1)}, f32[512]{0:T(512)}, u32[]{:S(2)}) copy-start(f32[512]{0:T(512)} %copy-done.72) | copy-start | bytes 6148
  1458.6 48.5 %copy-start.89 = (f32[512]{0:T(512)S(1)}, f32[512]{0:T(512)}, u32[]{:S(2)}) copy-start(f32[512]{0:T(512)} %copy-done.88) | copy-start | bytes 6148
  (92 other events, 617.5 us)
Sparse Core Ops, SparseCore 0:
  9.5 35.8 all-gather.16
  46.9 33.0 all-gather.10
  81.6 33.0 all-gather.14
  116.7 45.6 all-gather.18
  164.4 44.4 all-gather.12
  210.3 31.8 all-gather.20
  246.6 51.3 all-reduce.14
  306.8 45.7 all-gather.28
  354.8 44.4 all-gather.26
  411.1 50.1 all-reduce.16
  462.9 104.0 all-gather.22
  568.4 103.9 all-gather.24
  718.8 85.5 all-reduce.20
  834.1 43.7 reduce-scatter.12
  880.1 42.8 reduce-scatter.16
  925.1 42.8 reduce-scatter.10
  970.1 42.8 reduce-scatter.14
  1016.3 68.1 reduce-scatter.24
  1088.0 67.4 reduce-scatter.18
  1158.9 67.5 reduce-scatter.22
  1230.0 67.3 reduce-scatter.20
  1300.7 151.8 all-reduce.18
  1456.2 148.7 reduce-scatter.26
  1608.6 146.9 reduce-scatter.28
where the time goes:
time: 1770 us
  waiting for transfers between devices  1180 us (67%)
  matrix products  317 us (18%)
  other arithmetic  126 us (7%)
  blocking collectives  102 us (6%)
  local copies, waits for them, and re-layouts  21.5 us (1%)
    psum x1, waiting for transfers between devices, per_device(): lax.psum(jnp.dot(active, w_down, preferred_element_type=jnp.float32).asty...  153 us
    reduce_scatter x1, waiting for transfers between devices, per_device(): lax.psum_scatter(running[5].astype(jnp.bfloat16), ('fsdp', 'ctx'), scatte...  148 us
    psum x2, waiting for transfers between devices, per_device(): lax.psum(jnp.dot(attended, w_out, preferred_element_type=jnp.float32).ast...  99.8 us
    all_gather x1, waiting for transfers between devices, per_device(): lax.all_gather(up_weight, 'fsdp', axis=0, tiled=True)  99.3 us
    psum x1, waiting for transfers between devices, per_device(): lax.psum(times_transposed(grad_hidden, w_up).astype(jnp.bfloat16), 'tp')  85 us
    all_gather x2, waiting for transfers between devices, per_device(): lax.all_gather(keys_local, 'ctx', axis=0, tiled=True)  79.4 us
    dot_general x12, matrix products, inner_rows(): lax.dot_general(left, right, (((0,), (0,)), ((), ())), preferred_element_...  79.2 us
    reduce_scatter x1, waiting for transfers between devices, per_device(): lax.psum_scatter(running[4].astype(jnp.bfloat16), ('fsdp', 'ctx'), scatte...  79.1 us
  transfers between devices with their start and end apart: 24, of which 21 were waited for; matrix products, arithmetic and copies ran while one was open for 20% of the time, Pallas kernels for 0%

commit v1 on v0

--- a/solution.py
+++ b/solution.py
@@ -7,6 +7,19 @@
 
 HD = 128
 NEGATIVE = -1000000000.0
+
+
+def ring_gather(x, axis, dim):
+    ways = lax.axis_size(axis)
+    up = [(d, (d + 1) % ways) for d in range(ways)]
+    down = [(d, (d - 1) % ways) for d in range(ways)]
+    earlier, later = ([x], [x])
+    for _ in range(ways // 2):
+        earlier.append(lax.ppermute(earlier[-1], axis, up))
+    for _ in range((ways - 1) // 2):
+        later.append(lax.ppermute(later[-1], axis, down))
+    line = jnp.concatenate([*earlier[::-1], *later[1:]], axis=dim)
+    return jnp.roll(line, (lax.axis_index(axis) - ways // 2) * x.shape[dim], axis=dim)
 
 
 def norm_rows(values, gain, shift):
@@ -111,7 +124,7 @@
             jnp.dot(normed, w_value, preferred_element_type=jnp.float32) + value_bias
         ).astype(jnp.bfloat16)
         keys_tree, values_tree = (
-            lax.all_gather(keys_local, "ctx", axis=0, tiled=True),
+            ring_gather(keys_local, "ctx", 0),
             lax.all_gather(values_local, "ctx", axis=0, tiled=True),
         )
         tree_rows = keys_tree.shape[0]

time: 1770 us -> 1720 us (0.972)
  waiting for transfers between devices: 1180 us -> 1110 us
  other arithmetic: 126 us -> 145 us
    all_gather x2 -> x0, waiting for transfers between devices: 79.4 us -> none  [per_device(): lax.all_gather(keys_local, 'ctx', axis=0, tiled=True)]
    ppermute x0 -> x6, waiting for transfers between devices: none -> 62.5 us  [the longest x2 32.3 us: ring_gather(): later.append(lax.ppermute(later[-1], axis, down))]
    all_gather x2, waiting for transfers between devices: 52.1 us -> 12 us  [per_device(): lax.all_gather(values_local, 'ctx', axis=0, tiled=True)]
    all_gather x1, waiting for transfers between devices: 30.9 us -> 3.74 us  [per_device(): lax.all_gather(key_weight, 'fsdp', axis=0, tiled=True)]
    concatenate x0 -> x2, other arithmetic: none -> 19 us  [ring_gather(): jnp.roll(line, (lax.axis_index(axis) - ways // 2) * x.shape[dim], axis=dim)]
  transfers between devices with their start and end apart: 24 -> 28, of which waited for: 21 -> 23; matrix products, arithmetic and copies ran while one was open for 20% -> 21% of each run, Pallas kernels for 0% -> 0%
where the time goes in v1:
time: 1720 us
  waiting for transfers between devices  1110 us (65%)
  matrix products  313 us (18%)
  other arithmetic  145 us (8%)
  blocking collectives  103 us (6%)
  local copies, waits for them, and re-layouts  20.9 us (1%)
    psum x1, waiting for transfers between devices, per_device(): lax.psum(jnp.dot(active, w_down, preferred_element_type=jnp.float32).asty...  153 us
    reduce_scatter x1, waiting for transfers between devices, per_device(): lax.psum_scatter(running[5].astype(jnp.bfloat16), ('fsdp', 'ctx'), scatte...  148 us
    psum x2, waiting for transfers between devices, per_device(): lax.psum(jnp.dot(attended, w_out, preferred_element_type=jnp.float32).ast...  103 us
    all_gather x1, waiting for transfers between devices, per_device(): lax.all_gather(up_weight, 'fsdp', axis=0, tiled=True)  99.3 us
    psum x1, waiting for transfers between devices, per_device(): lax.psum(times_transposed(grad_hidden, w_up).astype(jnp.bfloat16), 'tp')  85 us
    reduce_scatter x1, waiting for transfers between devices, per_device(): lax.psum_scatter(running[4].astype(jnp.bfloat16), ('fsdp', 'ctx'), scatte...  79.2 us
    dot_general x12, matrix products, inner_rows(): lax.dot_general(left, right, (((0,), (0,)), ((), ())), preferred_element_...  79.2 us
    reduce_scatter x2, waiting for transfers between devices, per_device(): lax.psum_scatter(key_part.astype(jnp.bfloat16), 'ctx', scatter_dimension=...  72.3 us
  transfers between devices with their start and end apart: 28, of which 23 were waited for; matrix products, arithmetic and copies ran while one was open for 21% of the time, Pallas kernels for 0%

profile of v1, /device:TPU:0, one launch (start us, length us, event | category | flops | bytes accessed | tf_op | source)
XLA Modules:
  0.0 1719.1 jit_solution(1378138085236484588)
XLA Ops:
  14.6 30.8 %all-gather.9.cloned.1.call-done = bf16[2048,512]{1,0:T(8,128)(2,1)} async-done(((bf16[1024,512]{1,0:T(8,128)(2,1)}), bf16[2048,512]{1,0:T(8,128)(2,1)}) %all-gather.9.cloned.1.call-update) | async-done | bytes 2097168 | tf_op jit(solution)/shard_map/all_gather | solution.py:81
  49.7 13.3 all_gather.33
  63.0 13.2 all_gather.32
  87.7 13.0 collective-permute-done
  102.6 12.2 all-gather.13.cloned.1.call-done
  121.8 8.3 fusion.92
  133.0 9.2 fusion.176
  142.3 8.2 fusion
  150.5 11.9 all-gather.11.cloned.1.call-done
  162.4 8.8 fusion.141
  171.2 24.5 %all-gather.17.cloned.1.call-done = bf16[512,2048]{1,0:T(8,128)(2,1)} async-done(((bf16[512,1024]{1,0:T(8,128)(2,1)}), bf16[512,2048]{1,0:T(8,128)(2,1)}) %all-gather.17.cloned.1.call-update) | async-done | bytes 2097168 | tf_op jit(solution)/shard_map/all_gather | solution.py:82
  200.1 51.4 %all-reduce.15.cloned.1.call-done = bf16[512,2048]{1,0:T(8,128)(2,1)} async-done(((bf16[512,2048]{1,0:T(8,128)(2,1)}), bf16[512,2048]{1,0:T(8,128)(2,1)}) %all-reduce.15.cloned.1.call-update) | async-done | bytes 2097168 | tf_op jit(solution)/shard_map/psum | solution.py:157
  264.1 10.8 collective-permute-done.3
  283.1 32.3 %collective-permute-done.5 = bf16[512,512]{1,0:T(8,128)(2,1)} collective-permute-done((bf16[512,512]{1,0:T(8,128)(2,1)}, bf16[512,512]{1,0:T(8,128)(2,1)}, u32[]{:S(2)}, u32[]{:S(2)}) %collective-permute-start.5) | collective-permute-done | bytes 524320 | tf_op jit(solution)/shard_map/ppermute | solution.py:20
  318.4 10.7 fusion.85
  332.0 9.3 fusion.177
  349.5 8.6 fusion.138
  362.9 51.9 %all-reduce.17.cloned.1.call-done = bf16[512,2048]{1,0:T(8,128)(2,1)} async-done(((bf16[512,2048]{1,0:T(8,128)(2,1)}), bf16[512,2048]{1,0:T(8,128)(2,1)}) %all-reduce.17.cloned.1.call-update) | async-done | bytes 2097168 | tf_op jit(solution)/shard_map/psum | solution.py:157
  421.2 99.3 %all-gather.19.cloned.1.call-done = bf16[2048,2048]{1,0:T(8,128)(2,1)} async-done(((bf16[1024,2048]{1,0:T(8,128)(2,1)}), bf16[2048,2048]{1,0:T(8,128)(2,1)}) %all-gather.19.cloned.1.call-update) | async-done | bytes 8388624 | tf_op jit(solution)/shard_map/all_gather | solution.py:83
  530.7 26.2 %multiply_convert_fusion.5 = (bf16[512,2048]{1,0:T(8,128)(2,1)}, f32[512,2048]{1,0:T(8,128)}, bf16[512,2048]{1,0:T(8,128)(2,1)}, f32[512,2048]{1,0:T(8,128)}, f32[512,2048]{1,0:T(8,128)}) fusion(f32[2048]{0:T(1024)S(1)} %copy-done.103, f32[512,2048]{1,0:T(8,128)S(1)} %fusion.156, bf16[2048,2048]{1,0:T(8,128)(2,1)S(1)} %copy-done.101, ...), kind=kOutput, calls=%fused_computation.147 | convolution fusion | flops 4442816512 | bytes 33591296 | tf_op jit(solution)/shard_map/dot_general | solution.py:164
  556.9 68.9 %all-gather.21.cloned.1.call-done = bf16[2048,2048]{1,0:T(8,128)(2,1)} async-done(((bf16[2048,1024]{1,0:T(8,128)(2,1)}), bf16[2048,2048]{1,0:T(8,128)(2,1)}) %all-gather.21.cloned.1.call-update) | async-done | bytes 8388624 | tf_op jit(solution)/shard_map/all_gather | solution.py:84
  625.8 14.2 convert_reduce_fusion.8
  640.0 10.0 convolution_convert_fusion
  650.0 12.2 convert_reduce_fusion.9
  662.2 9.9 convolution_convert_fusion.1
  672.8 85.0 %all-reduce.21.cloned.1.call-done = (bf16[512,2048]{1,0:T(8,128)(2,1)}, bf16[512,2048]{1,0:T(8,128)(2,1)}) async-done(((bf16[512,2048]{1,0:T(8,128)(2,1)}, bf16[512,2048]{1,0:T(8,128)(2,1)}), (bf16[512,2048]{1,0:T(8,128)(2,1)}, bf16[512,2048]{1,0:T(8,128)(2,1)})) %all-reduce.21.cloned.1.call-update) | async-done | bytes 4194320 | tf_op jit(solution)/shard_map/psum | solution.py:182
  770.7 8.8 convert_reduce_fusion.10
  790.5 10.7 fusion.73
  801.3 11.3 multiply_reduce_fusion.1
  812.7 12.0 multiply_convert_fusion.1
  829.0 11.5 multiply_reduce_fusion
  840.5 11.9 multiply_convert_fusion
  889.8 31.6 %reduce-scatter.11.cloned.1.call-done = bf16[512,512]{0,1:T(8,128)(2,1)} async-done(((bf16[2048,512]{0,1:T(8,128)(2,1)}), bf16[512,512]{0,1:T(8,128)(2,1)}) %reduce-scatter.11.cloned.1.call-update) | async-done | bytes 524304 | tf_op jit(solution)/shard_map/reduce_scatter | solution.py:223
  925.8 40.6 %reduce-scatter.15.cloned.1.call-done = bf16[512,512]{0,1:T(8,128)(2,1)} async-done(((bf16[2048,512]{0,1:T(8,128)(2,1)}), bf16[512,512]{0,1:T(8,128)(2,1)}) %reduce-scatter.15.cloned.1.call-update) | async-done | bytes 524304 | tf_op jit(solution)/shard_map/reduce_scatter | solution.py:223
  972.7 9.2 convolution_convert_fusion.4
  981.9 9.3 convolution_convert_fusion.2
  1003.1 13.8 fusion.154
  1016.9 15.7 add_convert_fusion.1
  1034.2 9.9 fusion.112
  1044.1 11.0 add_convert_fusion
  1062.3 46.4 %reduce-scatter.19.cloned.1.call-done = bf16[256,512]{1,0:T(8,128)(2,1)} async-done(((bf16[2048,512]{1,0:T(8,128)(2,1)}), bf16[256,512]{1,0:T(8,128)(2,1)}) %reduce-scatter.19.cloned.1.call-update) | async-done | bytes 262160 | tf_op jit(solution)/shard_map/reduce_scatter | solution.py:269
  1110.5 35.6 %all-reduce.6 = (f32[512]{0:T(512)}, f32[512]{0:T(512)}, f32[2048]{0:T(1024)}) all-reduce(f32[512]{0:T(512)S(1)} %add_bitcast_fusion, f32[512]{0:T(512)S(1)} %add.362, f32[2048]{0:T(1024)S(1)} %add.368), channel_id=1, replica_groups=mesh['fsdp'=2,'ctx'=4,'tp'=4] {'fsdp','ctx'}, use_global_device_ids=true, to_apply=%region_47.49 | all-reduce | flops 3072 | bytes 24576 | tf_op jit(solution)/shard_map/psum | solution.py:306
  1146.1 33.8 %reduce-scatter.23.cloned.1.call-done = bf16[256,512]{1,0:T(8,128)(2,1)} async-done(((bf16[2048,512]{1,0:T(8,128)(2,1)}), bf16[256,512]{1,0:T(8,128)(2,1)}) %reduce-scatter.23.cloned.1.call-update) | async-done | bytes 262160 | tf_op jit(solution)/shard_map/reduce_scatter | solution.py:275
  1181.7 69.1 %reduce-scatter.21.cloned.1.call-done = bf16[256,512]{1,0:T(8,128)(2,1)} async-done(((bf16[2048,512]{1,0:T(8,128)(2,1)}), bf16[256,512]{1,0:T(8,128)(2,1)}) %reduce-scatter.21.cloned.1.call-update) | async-done | bytes 262160 | tf_op jit(solution)/shard_map/reduce_scatter | solution.py:272
  1252.6 153.3 %all-reduce.19.cloned.1.call-done = (bf16[512,2048]{1,0:T(8,128)(2,1)}, bf16[512,2048]{1,0:T(8,128)(2,1)}, bf16[512,2048]{1,0:T(8,128)(2,1)}, bf16[512,2048]{1,0:T(8,128)(2,1)}) async-done(((bf16[512,2048]{1,0:T(8,128)(2,1)}, bf16[512,2048]{1,0:T(8,128)(2,1)}, bf16[512,2048]{1,0:T(8,128)(2,1)}, bf16[512,2048]{1,0:T(8,128)(2,1)}), (bf16[512,2048]{1,0:T(8,128)(2,1)}, bf16[512,2048]{1,0:T(8,128)(2,1)}, ...) | async-done | bytes 8388624 | tf_op jit(solution)/shard_map/psum | solution.py:167
  1416.0 40.6 %all-reduce.7 = (bf16[2048]{0:T(1024)(128)(2,1)S(1)}, bf16[2048]{0:T(1024)(128)(2,1)S(1)}, bf16[2048]{0:T(1024)(128)(2,1)S(1)}, bf16[2048]{0:T(1024)(128)(2,1)S(...) all-reduce(bf16[2048]{0:T(1024)(128)(2,1)S(1)} %add_convert_fusion., ...), channel_id=6, replica_groups=mesh['fsdp'=2,'ctx'=4,'tp'=4] {'fsdp','ctx'}, use_global_device_ids=true, to_apply=%region_40.42.clone | all-reduce | flops 12288 | bytes 49152
  1479.3 79.2 %reduce-scatter.27.cloned.1.call-done = bf16[256,2048]{1,0:T(8,128)(2,1)} async-done(((bf16[2048,2048]{1,0:T(8,128)(2,1)}), bf16[256,2048]{1,0:T(8,128)(2,1)}) %reduce-scatter.27.cloned.1.call-update) | async-done | bytes 1048592 | tf_op jit(solution)/shard_map/reduce_scatter | solution.py:281
  1561.2 147.8 %reduce-scatter.29.cloned.1.call-done = bf16[2048,256]{1,0:T(8,128)(2,1)} async-done(((bf16[2048,2048]{1,0:T(8,128)(2,1)}), bf16[2048,256]{1,0:T(8,128)(2,1)}) %reduce-scatter.29.cloned.1.call-update) | async-done | bytes 1048592 | tf_op jit(solution)/shard_map/reduce_scatter | solution.py:284
  (395 shorter events, 235.1 us)
Async XLA Ops:
  7.2 38.2 %all-gather.9.cloned.1.call-start = ((), (), s32[]{:S(2)}) async-start(), calls=%async_computation.10 | async-start | bytes 3145728 | tf_op jit(solution)/shard_map/all_gather | solution.py:81
  7.9 72.1 %all-gather.15.cloned.1.call-start = ((), (), s32[]{:S(2)}) async-start(), calls=%async_computation.13 | async-start | bytes 3145728 | tf_op jit(solution)/shard_map/all_gather | solution.py:80
  8.7 106.0 %all-gather.13.cloned.1.call-start = ((), (), s32[]{:S(2)}) async-start(), calls=%async_computation.12 | async-start | bytes 3145728 | tf_op jit(solution)/shard_map/all_gather | solution.py:79
  9.4 153.0 %all-gather.11.cloned.1.call-start = ((), (), s32[]{:S(2)}) async-start(), calls=%async_computation.11 | async-start | bytes 2621440 | tf_op jit(solution)/shard_map/all_gather | solution.py:128
  12.9 36.1 %copy-start.63 = (f32[512]{0:T(512)}, f32[512]{0:T(512)S(1)}, u32[]{:S(2)}) copy-start(f32[512]{0:T(512)S(1)} %broadcast_multiply_fusion.3) | copy-start | bytes 6148
  13.6 35.4 %copy-start.92 = (f32[512]{0:T(512)}, f32[512]{0:T(512)S(1)}, u32[]{:S(2)}) copy-start(f32[512]{0:T(512)S(1)} %fusion.40) | copy-start | bytes 6148
  13.7 35.4 %copy-start.70 = (f32[512]{0:T(512)}, f32[512]{0:T(512)S(1)}, u32[]{:S(2)}) copy-start(f32[512]{0:T(512)S(1)} %fusion.148) | copy-start | bytes 6148
  14.5 100.2 %copy-start.27 = (bf16[512,2048]{1,0:T(8,128)(2,1)}, bf16[512,2048]{1,0:T(8,128)(2,1)S(1)}, u32[]{:S(2)}) copy-start(bf16[512,2048]{1,0:T(8,128)(2,1)S(1)} %fusion.33) | copy-start | bytes 6291460
  14.5 48.5 %copy-start.95 = (s32[2,512]{1,0:T(2,128)S(1)}, s32[2,512]{1,0:T(2,128)}, u32[]{:S(2)}) copy-start(s32[2,512]{1,0:T(2,128)} %param.24) | copy-start | bytes 12292
  14.5 61.7 %copy-start.100 = (s32[2,7]{1,0:T(2,128)S(1)}, s32[2,7]{1,0:T(2,128)}, u32[]{:S(2)}) copy-start(s32[2,7]{1,0:T(2,128)} %param.25) | copy-start | bytes 172
  49.1 146.7 %all-gather.17.cloned.1.call-start = ((), (), s32[]{:S(2)}) async-start(), calls=%async_computation.14 | async-start | bytes 3145728 | tf_op jit(solution)/shard_map/all_gather | solution.py:82
  49.6 201.8 %all-reduce.15.cloned.1.call-start = ((), (), s32[]{:S(2)}) async-start(), calls=%async_computation.15 | async-start | bytes 4194304 | tf_op jit(solution)/shard_map/psum | solution.py:157
  76.3 38.4 %copy-start.107 = (f32[512]{0:T(512)S(1)}, f32[512]{0:T(512)}, u32[]{:S(2)}) copy-start(f32[512]{0:T(512)} %param.29) | copy-start | bytes 6148
  83.7 17.0 collective-permute-start
  85.3 33.2 %collective-permute-start.2 = (bf16[512,512]{1,0:T(8,128)(2,1)}, bf16[512,512]{1,0:T(8,128)(2,1)}, u32[]{:S(2)}, u32[]{:S(2)}) collective-permute-start(bf16[512,512]{1,0:T(8,128)(2,1)} %convolution_convert_fusion.9), channel_id=1, source_target_pairs={{0,12},{4,0},{8,4},{12,8},{1,13},{5,1},{9,5},{13,9},{2,14},{6,2},{... | collective-permute-start | bytes 1572872 | tf_op jit(solution)/shard_map/ppermute | solution.py:20
  100.6 21.2 %collective-permute-start.1 = (bf16[512,512]{1,0:T(8,128)(2,1)}, bf16[512,512]{1,0:T(8,128)(2,1)}, u32[]{:S(2)}, u32[]{:S(2)}) collective-permute-start(bf16[512,512]{1,0:T(8,128)(2,1)} %collective-permute-done), channel_id=1, source_target_pairs={{0,4},{4,8},{8,12},{12,0},{1,5},{5,9},{9,13},{13,1},{2,6},{6,10},{... | collective-permute-start | bytes 1572872 | tf_op jit(solution)/shard_map/ppermute | solution.py:18
  171.2 80.3 %copy-start.53 = (f32[2048]{0:T(1024)S(1)}, f32[2048]{0:T(1024)}, u32[]{:S(2)}) copy-start(f32[2048]{0:T(1024)} %param.34) | copy-start | bytes 24580
  199.9 55.9 %copy-start.37 = (bf16[2048,512]{1,0:T(8,128)(2,1)S(1)}, bf16[2048,512]{1,0:T(8,128)(2,1)}, u32[]{:S(2)}) copy-start(bf16[2048,512]{1,0:T(8,128)(2,1)} %all-gather.15.cloned.1.call-done) | copy-start | bytes 6291460
  200.0 149.5 %all-gather.23.cloned.1.call-start = ((), (), s32[]{:S(2)}) async-start(), calls=%async_computation.18 | async-start | bytes 2621440 | tf_op jit(solution)/shard_map/all_gather | solution.py:128
  200.1 79.0 %copy-start.65 = (f32[512]{0:T(512)}, f32[512]{0:T(512)S(1)}, u32[]{:S(2)}) copy-start(f32[512]{0:T(512)S(1)} %broadcast_multiply_fusion.1) | copy-start | bytes 6148
  258.0 17.0 collective-permute-start.3
  259.5 55.8 %collective-permute-start.5 = (bf16[512,512]{1,0:T(8,128)(2,1)}, bf16[512,512]{1,0:T(8,128)(2,1)}, u32[]{:S(2)}, u32[]{:S(2)}) collective-permute-start(bf16[512,512]{1,0:T(8,128)(2,1)} %convolution_convert_fusion.8), channel_id=1, source_target_pairs={{0,12},{4,0},{8,4},{12,8},{1,13},{5,1},{9,5},{13,9},{2,14},{6,2},{... | collective-permute-start | bytes 1572872 | tf_op jit(solution)/shard_map/ppermute | solution.py:20
  264.1 150.7 %all-reduce.17.cloned.1.call-start = ((), (), s32[]{:S(2)}) async-start(), calls=%async_computation.19 | async-start | bytes 4194304 | tf_op jit(solution)/shard_map/psum | solution.py:157
  274.9 43.5 %collective-permute-start.4 = (bf16[512,512]{1,0:T(8,128)(2,1)}, bf16[512,512]{1,0:T(8,128)(2,1)S(1)}, u32[]{:S(2)}, u32[]{:S(2)}) collective-permute-start(bf16[512,512]{1,0:T(8,128)(2,1)} %collective-permute-done.3), channel_id=1, source_target_pairs={{0,4},{4,8},{8,12},{12,0},{1,5},{5,9},{9,13},{13,1},{2,6},{6,10},{... | collective-permute-start | bytes 1572872 | tf_op jit(solution)/shard_map/ppermute | solution.py:18
  361.5 158.9 %all-gather.19.cloned.1.call-start = ((), (), s32[]{:S(2)}) async-start(), calls=%async_computation.16 | async-start | bytes 12582912 | tf_op jit(solution)/shard_map/all_gather | solution.py:83
  362.2 263.6 %all-gather.21.cloned.1.call-start = ((), (), s32[]{:S(2)}) async-start(), calls=%async_computation.17 | async-start | bytes 12582912 | tf_op jit(solution)/shard_map/all_gather | solution.py:84
  362.8 394.9 %all-reduce.21.cloned.1.call-start = ((), (), s32[]{:S(2)}) async-start(), calls=%async_computation.31 | async-start | bytes 8388608 | tf_op jit(solution)/shard_map/psum | solution.py:182
  419.3 101.2 %copy-start.58 = (f32[2048]{0:T(1024)S(1)}, f32[2048]{0:T(1024)}, u32[]{:S(2)}) copy-start(f32[2048]{0:T(1024)} %param.35) | copy-start | bytes 24580
  419.3 101.2 %copy-start.104 = (f32[2048]{0:T(1024)S(1)}, f32[2048]{0:T(1024)}, u32[]{:S(2)}) copy-start(f32[2048]{0:T(1024)} %param.36) | copy-start | bytes 24580
  419.3 351.3 %copy-start.61 = (f32[512]{0:T(512)}, f32[512]{0:T(512)S(1)}, u32[]{:S(2)}) copy-start(f32[512]{0:T(512)S(1)} %get-tuple-element.105) | copy-start | bytes 6148
  421.2 349.5 %copy-start.76 = (f32[512]{0:T(512)}, f32[512]{0:T(512)S(1)}, u32[]{:S(2)}) copy-start(f32[512]{0:T(512)S(1)} %fusion.151) | copy-start | bytes 6148
  421.2 109.5 %copy-start.103 = (f32[2048]{0:T(1024)S(1)}, f32[2048]{0:T(1024)}, u32[]{:S(2)}) copy-start(f32[2048]{0:T(1024)} %param.38) | copy-start | bytes 24580
  672.1 207.4 %reduce-scatter.13.cloned.1.call-start = ((), (), s32[]{:S(2)}) async-start(), calls=%async_computation.21 | async-start | bytes 2621440 | tf_op jit(solution)/shard_map/reduce_scatter | solution.py:226
  787.4 96.5 %reduce-scatter.17.cloned.1.call-start = ((), (), s32[]{:S(2)}) async-start(), calls=%async_computation.23 | async-start | bytes 2621440 | tf_op jit(solution)/shard_map/reduce_scatter | solution.py:226
  801.3 120.2 %reduce-scatter.11.cloned.1.call-start = ((), (), s32[]{:S(2)}) async-start(), calls=%async_computation.20 | async-start | bytes 2621440 | tf_op jit(solution)/shard_map/reduce_scatter | solution.py:223
  828.9 137.6 %reduce-scatter.15.cloned.1.call-start = ((), (), s32[]{:S(2)}) async-start(), calls=%async_computation.22 | async-start | bytes 2621440 | tf_op jit(solution)/shard_map/reduce_scatter | solution.py:223
  856.9 203.6 %reduce-scatter.25.cloned.1.call-start = ((), (), s32[]{:S(2)}) async-start(), calls=%async_computation.27 | async-start | bytes 2359296 | tf_op jit(solution)/shard_map/reduce_scatter | solution.py:278
  861.4 247.4 %reduce-scatter.19.cloned.1.call-start = ((), (), s32[]{:S(2)}) async-start(), calls=%async_computation.24 | async-start | bytes 2359296 | tf_op jit(solution)/shard_map/reduce_scatter | solution.py:269
  879.4 300.5 %reduce-scatter.23.cloned.1.call-start = ((), (), s32[]{:S(2)}) async-start(), calls=%async_computation.26 | async-start | bytes 2359296 | tf_op jit(solution)/shard_map/reduce_scatter | solution.py:275
  889.8 361.0 %reduce-scatter.21.cloned.1.call-start = ((), (), s32[]{:S(2)}) async-start(), calls=%async_computation.25 | async-start | bytes 2359296 | tf_op jit(solution)/shard_map/reduce_scatter | solution.py:272
  925.8 46.8 %copy-start.109 = (bf16[512,2048]{1,0:T(8,128)(2,1)S(1)}, bf16[512,2048]{1,0:T(8,128)(2,1)}, u32[]{:S(2)}) copy-start(bf16[512,2048]{1,0:T(8,128)(2,1)} %get-tuple-element.65) | copy-start | bytes 6291460
  972.4 433.5 %all-reduce.19.cloned.1.call-start = ((), (), s32[]{:S(2)}) async-start(), calls=%async_computation.30 | async-start | bytes 16777216 | tf_op jit(solution)/shard_map/psum | solution.py:167
  1002.5 556.0 %reduce-scatter.27.cloned.1.call-start = ((), (), s32[]{:S(2)}) async-start(), calls=%async_computation.28 | async-start | bytes 9437184 | tf_op jit(solution)/shard_map/reduce_scatter | solution.py:281
  1032.6 676.5 %reduce-scatter.29.cloned.1.call-start = ((), (), s32[]{:S(2)}) async-start(), calls=%async_computation.29 | async-start | bytes 9437184 | tf_op jit(solution)/shard_map/reduce_scatter | solution.py:284
  1411.9 48.5 %copy-start.15 = (bf16[512,2048]{1,0:T(8,128)(2,1)S(1)}, bf16[512,2048]{1,0:T(8,128)(2,1)}, u32[]{:S(2)}) copy-start(bf16[512,2048]{1,0:T(8,128)(2,1)} %all-reduce.15.cloned.1.call-done) | copy-start | bytes 6291460
  1411.9 48.5 %copy-start.67 = (f32[2048]{0:T(1024)S(1)}, f32[2048]{0:T(1024)}, u32[]{:S(2)}) copy-start(f32[2048]{0:T(1024)} %param.40) | copy-start | bytes 24580
  1411.9 48.5 %copy-start.75 = (f32[512]{0:T(512)S(1)}, f32[512]{0:T(512)}, u32[]{:S(2)}) copy-start(f32[512]{0:T(512)} %copy-done.74) | copy-start | bytes 6148
  1411.9 48.5 %copy-start.91 = (f32[512]{0:T(512)S(1)}, f32[512]{0:T(512)}, u32[]{:S(2)}) copy-start(f32[512]{0:T(512)} %copy-done.90) | copy-start | bytes 6148
  (98 other events, 766.8 us)
Sparse Core Ops, SparseCore 0:
  9.5 35.8 all-gather.8
  46.9 33.0 all-gather.14
  81.6 33.0 all-gather.12
  116.7 45.6 all-gather.10
  163.8 31.8 all-gather.16
  200.1 51.3 all-reduce.14
  264.2 65.8 all-gather.22
  361.6 53.0 all-reduce.16
  416.3 104.0 all-gather.18
  521.8 103.9 all-gather.20
  672.2 85.4 all-reduce.20
  787.5 43.7 reduce-scatter.12
  833.6 42.8 reduce-scatter.16
  878.6 42.8 reduce-scatter.10
  923.6 42.8 reduce-scatter.14
  969.9 67.9 reduce-scatter.24
  1041.3 67.4 reduce-scatter.18
  1112.1 67.7 reduce-scatter.22
  1183.5 67.3 reduce-scatter.20
  1253.9 151.9 all-reduce.18
  1409.6 148.8 reduce-scatter.26
  1562.1 146.9 reduce-scatter.28
